TPU v7x, 512 devices: a whole 4x8x8 slice. The times are simulated.
512 devices in a mesh: head: 8 (over z), tok: 64 (over x, y, core).
Axes of the slice: x: 4, y: 8, z: 8, core: 2. Of those that a mesh axis runs over, the one named last changes fastest.
Arguments:
- patches: bfloat16 [32768, 1280], P('tok')
- row_table: bfloat16 [64, 1280], replicated, may hold values from -0.59765625 to 0.59765625
- col_table: bfloat16 [64, 1280], replicated, may hold values from -0.59765625 to 0.59765625
- qkv_weight: bfloat16 [3, 1280, 1280], P(None, 'head'), may hold values from -0.15625 to 0.15625
- out_weight: bfloat16 [1280, 1280], P('head'), may hold values from -0.15625 to 0.15625
- merge_weight: bfloat16 [1280, 5120], P('head'), may hold values from -0.078125 to 0.078125
- segment_ids: int32 [32768], P('tok'), may hold values from 0 to 63, as said below
- image_grids: int32 [64, 2], replicated, may hold values from 2 to 62, as said below
- image_offsets: int32 [64], replicated, may hold values from 0 to 32736, as said below
- owners: int32 [64], replicated, may hold values from 0 to 63, each once
Outputs:
- delivered: bfloat16 [15872, 1280], P('tok', 'head')
Inputs may be any that keep to these rules, and one draw needn't show every extreme that they name: `segment_ids`: tokens of each image are consecutive and images follow in order; the pair p of token blocks (tokens 2 * p * 512 to 2 * (p + 1) * 512 - 1) holds exactly images 2 * p and 2 * p + 1, with no padding. `image_grids`: heights are even, widths are 16, and height times width is the image's token count. Within an image each 2x2 window of patches is four consecutive tokens (top left, top right, bottom left, bottom right), windows in row-major order. The longest image has exactly 992 tokens. `image_offsets`: the first token of each image, consistent with segment_ids. `owners`: every device index along tok owns exactly one image.
All inputs are finite; a program needn't handle non-finite values.
Results may differ from a plain program's by a relative error of at most 0.019.
Values may be sent and summed in bfloat16 or wider, within the bound.
No kernel may reach another device: no remote copies, remote signals or barrier semaphores. Data moves between devices by JAX's collectives and lax.ppermute only.
A program may use at most 64 MiB of HBM per device.

v0:
```python
import math
import jax
import jax.numpy as jnp
from jax import lax
from jax.sharding import PartitionSpec as P

HEAD_DIM = 80
CAP = 248


def partner(x, axis, apart):
    return lax.ppermute(x, axis, [(i, i ^ 1 << apart) for i in range(lax.axis_size(axis))])


def layer_norm(values):
    centered = values - jnp.mean(values, axis=-1, keepdims=True)
    variance = jnp.mean(centered * centered, axis=-1, keepdims=True)
    return centered * lax.rsqrt(variance + 1e-06)


def grid_place(token_pos, start_tok, width_now):
    local_pos = token_pos - start_tok
    window = local_pos // 4
    quarter = local_pos % 4
    half_width = jnp.maximum(width_now // 2, 1)
    row_index = 2 * (window // half_width) + quarter // 2
    col_index = 2 * (window % half_width) + quarter % 2
    return (row_index, col_index)


def dot_last(left, right):
    return lax.dot_general(
        left, right, (((1,), (1,)), ((), ())), preferred_element_type=jnp.float32
    )


def on_device(
    patches,
    row_table,
    col_table,
    qkv_weight,
    out_weight,
    merge_weight,
    segment_ids,
    image_grids,
    image_offsets,
    owners,
):
    block_rows = patches.shape[0]
    width_here = qkv_weight.shape[1]
    heads_here = width_here // HEAD_DIM
    image_count = owners.shape[0]
    image_ids = jnp.arange(image_count, dtype=jnp.int32)
    token_pos = lax.axis_index("tok") * block_rows + jnp.arange(block_rows, dtype=jnp.int32)
    member = segment_ids[:, None] == image_ids[None, :]
    start_tok = jnp.sum(jnp.where(member, image_offsets[None, :], 0), axis=1)
    width_now = jnp.sum(jnp.where(member, image_grids[None, :, 1], 0), axis=1)
    row_index, col_index = grid_place(token_pos, start_tok, width_now)
    side_ids = jnp.arange(row_table.shape[0], dtype=jnp.int32)
    row_onehot = (row_index[:, None] == side_ids[None, :]).astype(jnp.bfloat16)
    col_onehot = (col_index[:, None] == side_ids[None, :]).astype(jnp.bfloat16)
    resid = (
        patches.astype(jnp.float32)
        + jnp.dot(row_onehot, row_table, preferred_element_type=jnp.float32)
        + jnp.dot(col_onehot, col_table, preferred_element_type=jnp.float32)
    )
    normed = layer_norm(resid).astype(jnp.bfloat16)
    query_rows = dot_last(normed, qkv_weight[0]).astype(jnp.bfloat16)
    key_rows = dot_last(normed, qkv_weight[1]).astype(jnp.bfloat16)
    value_rows = dot_last(normed, qkv_weight[2]).astype(jnp.bfloat16)
    seg_wire = segment_ids.astype(jnp.bfloat16)
    far_keys, far_values, far_seg = partner((key_rows, value_rows, seg_wire), "tok", 0)
    query_heads = query_rows.reshape(block_rows, heads_here, HEAD_DIM)
    key_heads = jnp.concatenate([key_rows, far_keys], axis=0).reshape(
        2 * block_rows, heads_here, HEAD_DIM
    )
    value_heads = jnp.concatenate([value_rows, far_values], axis=0).reshape(
        2 * block_rows, heads_here, HEAD_DIM
    )
    query_seg = seg_wire.astype(jnp.float32)
    key_seg = jnp.concatenate([seg_wire, far_seg], axis=0).astype(jnp.float32)
    scores = jnp.einsum(
        "qhd,khd->hqk", query_heads, key_heads, preferred_element_type=jnp.float32
    ) * (1.0 / math.sqrt(HEAD_DIM))
    same_image = query_seg[:, None] == key_seg[None, :]
    raw_weights = jnp.where(same_image[None], jnp.exp(scores), 0.0)
    weight_sum = jnp.sum(raw_weights, axis=-1, keepdims=True)
    attn_probs = (raw_weights / weight_sum).astype(jnp.bfloat16)
    mixed = jnp.einsum("hqk,khd->qhd", attn_probs, value_heads, preferred_element_type=jnp.float32)
    attended = mixed.reshape(block_rows, width_here).astype(jnp.bfloat16)
    partial_sum = jnp.dot(attended, out_weight, preferred_element_type=jnp.float32)
    head_total = lax.psum(partial_sum.astype(jnp.bfloat16), "head").astype(jnp.float32)
    normed_two = layer_norm(resid + head_total).astype(jnp.bfloat16)
    merged = normed_two.reshape(block_rows // 4, 4 * normed_two.shape[1])
    projected = dot_last(merged, merge_weight).astype(jnp.bfloat16)
    owner_mask = owners == lax.axis_index("tok")
    image_id = jnp.sum(jnp.where(owner_mask, image_ids, 0))
    chosen = image_ids == image_id
    first_row = jnp.sum(jnp.where(chosen, image_offsets, 0)) // 4
    merged_count = jnp.sum(jnp.where(chosen, image_grids[:, 0] * image_grids[:, 1], 0)) // 4
    slot_ids = jnp.arange(CAP, dtype=jnp.int32)
    piece_rows = lax.all_gather(projected, "tok", axis=0, tiled=True)
    row_ids = jnp.arange(piece_rows.shape[0], dtype=jnp.int32)
    slot_of = row_ids - first_row
    inside = row_ids < first_row + merged_count
    selector = (slot_of[None, :] == slot_ids[:, None]) & inside[None, :]
    owner_rows = jnp.dot(
        selector.astype(jnp.bfloat16), piece_rows, preferred_element_type=jnp.float32
    )
    return owner_rows.astype(jnp.bfloat16)


def solution(mesh):
    placed = (
        P("tok", None),
        P(),
        P(),
        P(None, "head", None),
        P("head", None),
        P("head", None),
        P("tok"),
        P(),
        P(),
        P(),
    )
    return jax.shard_map(
        on_device, mesh=mesh, in_specs=placed, out_specs=P("tok", "head"), check_vma=False
    )
```

profile of v0, /device:TPU:1, one launch (start us, length us, event | category | flops | bytes accessed | tf_op | source)
XLA Modules:
  0.0 213.2 jit_solution(1868882156168978352)
XLA Ops:
  6.5 0.8 slice_bitcast_fusion
  7.4 0.8 select_reduce_fusion
  8.1 0.1 fusion.25
  8.3 2.0 convolution_add_fusion.1
  10.3 0.6 fusion.36
  10.9 0.4 multiply_reduce_fusion.1
  11.4 0.3 multiply_convert_fusion.1
  11.7 0.7 copy-done.1
  12.4 0.7 copy-done.9
  13.1 0.6 convolution_convert_fusion.3
  13.7 8.8 %collective-permute-start = (bf16[512,160]{0,1:T(8,128)(2,1)S(1)}, bf16[512,160]{0,1:T(8,128)(2,1)S(1)}, u32[]{:S(2)}, u32[]{:S(2)}) collective-permute-start(bf16[512,160]{0,1:T(8,128)(2,1)S(1)} %convolution_convert_fusion.3), channel_id=1, source_target_pairs={{0,1},{1,0},{2,3},{3,2},{4,5},{5,4},{6,7},{7,6},{8,9},{9,8},{10,11... | collective-permute-start | bytes 491528 | tf_op jit(solution)/shard_map/ppermute | solution.py:12
  22.5 1.9 collective-permute-start.1
  24.5 0.6 convolution_convert_fusion.1
  25.0 2.4 %collective-permute-start.2 = (bf16[512,160]{0,1:T(8,128)(2,1)S(1)}, bf16[512,160]{0,1:T(8,128)(2,1)S(1)}, u32[]{:S(2)}, u32[]{:S(2)}) collective-permute-start(bf16[512,160]{0,1:T(8,128)(2,1)S(1)} %convolution_convert_fusion.1), channel_id=1, source_target_pairs={{0,1},{1,0},{2,3},{3,2},{4,5},{5,4},{6,7},{7,6},{8,9},{9,8},{10,11... | collective-permute-start | bytes 491528 | tf_op jit(solution)/shard_map/ppermute | solution.py:12
  27.5 0.6 convolution_convert_fusion.2
  28.1 0.4 broadcast_compare_fusion
  28.5 1.5 fusion.5
  30.0 1.4 fusion.7
  31.4 1.6 convolution_convert_fusion
  33.1 0.0 all-gather.2.cloned.1.call-start
  33.1 78.2 %all-reduce.2.cloned.1.call-done = bf16[512,1280]{1,0:T(8,128)(2,1)} async-done(((bf16[512,1280]{1,0:T(8,128)(2,1)}), bf16[512,1280]{1,0:T(8,128)(2,1)}) %all-reduce.2.cloned.1.call-update) | async-done | bytes 1310736 | tf_op jit(solution)/shard_map/psum | solution.py:92
  111.4 2.6 %fusion.11 = f32[512]{0:T(512)S(1)} fusion(f32[512,1280]{1,0:T(8,128)} %copy-done.1, bf16[512,1280]{1,0:T(8,128)(2,1)} %all-reduce.2.cloned.1.call-done), kind=kLoop, calls=%fused_computation.24 | loop fusion | flops 1965568 | bytes 3934208 | tf_op jit(solution)/shard_map/reduce_sum | solution.py:16
  114.0 0.3 copy-done.2
  114.3 0.4 copy-done.3
  114.6 0.5 multiply_reduce_fusion
  115.2 1.5 multiply_convert_fusion
  116.7 2.5 %reshape.198 = bf16[128,5120]{1,0:T(8,128)(2,1)S(1)} reshape(bf16[512,1280]{1,0:T(8,128)(2,1)} %multiply_convert_fusion) | data formatting | bytes 2621440 | tf_op jit(solution)/shard_map/reshape | solution.py:94
  119.2 1.2 convolution_convert_fusion.4
  120.5 0.6 fusion.32
  121.1 1.3 fusion.30
  127.3 74.8 %all-gather.2.cloned.1.call-done = bf16[8192,160]{0,1:T(8,128)(2,1)} async-done(((bf16[128,160]{0,1:T(8,128)(2,1)}), bf16[8192,160]{0,1:T(8,128)(2,1)}) %all-gather.2.cloned.1.call-update) | async-done | bytes 2621456 | tf_op jit(solution)/shard_map/all_gather | solution.py:102
  202.1 4.3 %fusion.8 = bf16[248,160]{0,1:T(8,128)(2,1)} fusion(bf16[8192,160]{0,1:T(8,128)(2,1)} %all-gather.2.cloned.1.call-done, s32[8192]{0:T(1024)S(1)} %iota_subtract_fusion, pred[8192]{0:T(1024)(128)(4,1)S(1)} %iota_compare_fusion.6), kind=kOutput, calls=%fused_computation.21 | convolution fusion | flops 654220032 | bytes 2741760 | tf_op jit(solution)/shard_map/dot_general | solution.py:107
  (34 shorter events, 0.2 us)
Async XLA Ops:
  6.5 112.7 %copy-start = (bf16[160,5120]{1,0:T(8,128)(2,1)S(1)}, bf16[160,5120]{1,0:T(8,128)(2,1)}, u32[]{:S(2)}) copy-start(bf16[160,5120]{1,0:T(8,128)(2,1)} %param.15) | copy-start | bytes 4915204
  6.5 3.7 %copy-start.5 = (bf16[64,1280]{1,0:T(8,128)(2,1)S(1)}, bf16[64,1280]{1,0:T(8,128)(2,1)}, u32[]{:S(2)}) copy-start(bf16[64,1280]{1,0:T(8,128)(2,1)} %param.12) | copy-start | bytes 491524
  6.5 104.8 %all-reduce.2.cloned.1.call-start = ((), (), s32[]{:S(2)}) async-start(), calls=%async_computation | async-start | bytes 2621440 | tf_op jit(solution)/shard_map/psum | solution.py:92
  10.9 1.5 copy-start.1
  11.3 1.8 copy-start.9
  11.4 11.2 %copy-start.6 = (s32[512]{0:T(512)S(1)}, s32[512]{0:T(512)}, u32[]{:S(2)}) copy-start(s32[512]{0:T(512)} %param.16) | copy-start | bytes 6148
  13.7 16.3 %collective-permute-start = (bf16[512,160]{0,1:T(8,128)(2,1)S(1)}, bf16[512,160]{0,1:T(8,128)(2,1)S(1)}, u32[]{:S(2)}, u32[]{:S(2)}) collective-permute-start(bf16[512,160]{0,1:T(8,128)(2,1)S(1)} %convolution_convert_fusion.3), channel_id=1, source_target_pairs={{0,1},{1,0},{2,3},{3,2},{4,5},{5,4},{6,7},{7,6},{8,9},{9,8},{10,11... | collective-permute-start | bytes 491528 | tf_op jit(solution)/shard_map/ppermute | solution.py:12
  22.5 5.5 %collective-permute-start.1 = (bf16[512]{0:T(512)(128)(2,1)S(1)}, bf16[512]{0:T(512)(128)(2,1)S(1)}, u32[]{:S(2)}, u32[]{:S(2)}) collective-permute-start(bf16[512]{0:T(512)(128)(2,1)S(1)} %get-tuple-element.8), channel_id=1, source_target_pairs={{0,1},{1,0},{2,3},{3,2},{4,5},{5,4},{6,7},{7,6},{8,9},{9,8},{10,11... | collective-permute-start | bytes 3080 | tf_op jit(solution)/shard_map/ppermute | solution.py:12
  25.0 3.4 %collective-permute-start.2 = (bf16[512,160]{0,1:T(8,128)(2,1)S(1)}, bf16[512,160]{0,1:T(8,128)(2,1)S(1)}, u32[]{:S(2)}, u32[]{:S(2)}) collective-permute-start(bf16[512,160]{0,1:T(8,128)(2,1)S(1)} %convolution_convert_fusion.1), channel_id=1, source_target_pairs={{0,1},{1,0},{2,3},{3,2},{4,5},{5,4},{6,7},{7,6},{8,9},{9,8},{10,11... | collective-permute-start | bytes 491528 | tf_op jit(solution)/shard_map/ppermute | solution.py:12
  30.0 1.4 copy-start.4
  33.1 169.0 %all-gather.2.cloned.1.call-start = ((), (), s32[]{:S(2)}) async-start(), calls=%async_computation.1 | async-start | bytes 2662400 | tf_op jit(solution)/shard_map/all_gather | solution.py:102
  111.4 2.9 %copy-start.2 = (f32[512,1280]{1,0:T(8,128)S(1)}, f32[512,1280]{1,0:T(8,128)}, u32[]{:S(2)}) copy-start(f32[512,1280]{1,0:T(8,128)} %copy-done.1) | copy-start | bytes 7864324
  111.4 3.3 %copy-start.3 = (bf16[512,1280]{1,0:T(8,128)(2,1)S(1)}, bf16[512,1280]{1,0:T(8,128)(2,1)}, u32[]{:S(2)}) copy-start(bf16[512,1280]{1,0:T(8,128)(2,1)} %all-reduce.2.cloned.1.call-done) | copy-start | bytes 3932164
  116.7 3.8 %copy-start.10 = (s32[64]{0:T(128)S(1)}, s32[64]{0:T(128)}, u32[]{:S(2)}) copy-start(s32[64]{0:T(128)} %param.19) | copy-start | bytes 772
  116.7 4.4 %copy-start.7 = (s32[64]{0:T(128)S(1)}, s32[64]{0:T(128)}, u32[]{:S(2)}) copy-start(s32[64]{0:T(128)} %param.18) | copy-start | bytes 772
  116.7 4.4 %copy-start.8 = (s32[64,2]{0,1:T(2,128)S(1)}, s32[64,2]{0,1:T(2,128)}, u32[]{:S(2)}) copy-start(s32[64,2]{0,1:T(2,128)} %param.17) | copy-start | bytes 1540
Sparse Core Ops, SparseCore 0:
  33.2 78.1 all-reduce.1
  120.6 81.4 all-gather.1
where the time goes:
time: 214 us; the launch traced here: 213 us
  waiting for transfers between devices  153 us (71%)
  between operations  18.4 us (9%)
  matrix products  14.4 us (7%)
  starting transfers between devices  13.2 us (6%)
  other arithmetic  8.66 us (4%)
  local copies, waits for them, and re-layouts  5.5 us (3%)
    psum x1, waiting for transfers between devices, on_device(): lax.psum(partial_sum.astype(jnp.bfloat16), 'head').astype(jnp.float32)  78.2 us
    all_gather x1, waiting for transfers between devices, on_device(): piece_rows = lax.all_gather(projected, 'tok', axis=0, tiled=True)  74.8 us
    ppermute x3, starting transfers between devices, partner(): lax.ppermute(x, axis, [(i, i ^ 1 << apart) for i in range(lax.axis_size(a...  13.1 us
    dot_general x1, matrix products, on_device(): jnp.dot(selector.astype(jnp.bfloat16), piece_rows, preferred_element_type...  4.35 us
  transfers between devices with their start and end apart: 5, of which 2 were waited for; matrix products, arithmetic and copies ran while one was open for 2% of the time, Pallas kernels for 0%

commit v1 on v0

--- a/solution.py
+++ b/solution.py
@@ -89,7 +89,9 @@
     mixed = jnp.einsum("hqk,khd->qhd", attn_probs, value_heads, preferred_element_type=jnp.float32)
     attended = mixed.reshape(block_rows, width_here).astype(jnp.bfloat16)
     partial_sum = jnp.dot(attended, out_weight, preferred_element_type=jnp.float32)
-    head_total = lax.psum(partial_sum.astype(jnp.bfloat16), "head").astype(jnp.float32)
+    head_total = jnp.sum(lax.all_gather(partial_sum.astype(jnp.bfloat16), "head"), axis=0).astype(
+        jnp.float32
+    )
     normed_two = layer_norm(resid + head_total).astype(jnp.bfloat16)
     merged = normed_two.reshape(block_rows // 4, 4 * normed_two.shape[1])
     projected = dot_last(merged, merge_weight).astype(jnp.bfloat16)

time: 214 us -> 253 us (1.18)
  waiting for transfers between devices: 153 us -> 187 us
  other arithmetic: 8.66 us -> 14.6 us
    all_gather x0 -> x1, waiting for transfers between devices: none -> 116 us  [on_device(): lax.all_gather(partial_sum.astype(jnp.bfloat16), 'head')]
    psum x1 -> x0, waiting for transfers between devices: 78.2 us -> none  [on_device(): lax.psum(partial_sum.astype(jnp.bfloat16), 'head').astype(jnp.float32)]
    reduce_sum x0 -> x1, other arithmetic: none -> 6.23 us  [on_device(): jnp.sum(lax.all_gather(partial_sum.astype(jnp.bfloat16), 'head'), axis=0)]
    all_gather x1, waiting for transfers between devices: 74.8 us -> 70.6 us  [on_device(): piece_rows = lax.all_gather(projected, 'tok', axis=0, tiled=True)]
where the time goes in v1:
time: 253 us; the launch traced here: 252 us
  waiting for transfers between devices  187 us (74%)
  between operations  18.5 us (7%)
  other arithmetic  14.6 us (6%)
  matrix products  14.4 us (6%)
  starting transfers between devices  13.3 us (5%)
  local copies, waits for them, and re-layouts  5.1 us (2%)
    all_gather x1, waiting for transfers between devices, on_device(): lax.all_gather(partial_sum.astype(jnp.bfloat16), 'head')  116 us
    all_gather x1, waiting for transfers between devices, on_device(): piece_rows = lax.all_gather(projected, 'tok', axis=0, tiled=True)  70.6 us
    ppermute x3, starting transfers between devices, partner(): lax.ppermute(x, axis, [(i, i ^ 1 << apart) for i in range(lax.axis_size(a...  13.1 us
    reduce_sum x1, other arithmetic, on_device(): jnp.sum(lax.all_gather(partial_sum.astype(jnp.bfloat16), 'head'), axis=0)  6.23 us
  transfers between devices with their start and end apart: 5, of which 2 were waited for; matrix products, arithmetic and copies ran while one was open for 2% of the time, Pallas kernels for 0%

profile of v1, /device:TPU:1, one launch (start us, length us, event | category | flops | bytes accessed | tf_op | source)
XLA Modules:
  0.0 252.4 jit_solution(289164897657811070)
XLA Ops:
  6.5 0.8 slice_bitcast_fusion
  7.4 0.8 select_reduce_fusion
  8.1 0.1 fusion.25
  8.3 2.0 convolution_add_fusion.1
  10.3 0.6 fusion.36
  10.9 0.4 multiply_reduce_fusion.1
  11.4 0.3 multiply_convert_fusion.1
  11.7 0.8 copy-done.1
  12.4 0.7 copy-done.8
  13.1 0.6 convolution_convert_fusion.1
  13.7 8.8 %collective-permute-start.2 = (bf16[512,160]{0,1:T(8,128)(2,1)S(1)}, bf16[512,160]{0,1:T(8,128)(2,1)S(1)}, u32[]{:S(2)}, u32[]{:S(2)}) collective-permute-start(bf16[512,160]{0,1:T(8,128)(2,1)S(1)} %convolution_convert_fusion.1), channel_id=1, source_target_pairs={{0,1},{1,0},{2,3},{3,2},{4,5},{5,4},{6,7},{7,6},{8,9},{9,8},{10,11... | collective-permute-start | bytes 491528 | tf_op jit(solution)/shard_map/ppermute | solution.py:12
  22.5 1.9 collective-permute-start.1
  24.5 0.6 convolution_convert_fusion.3
  25.0 2.4 collective-permute-start
  27.5 0.6 convolution_convert_fusion.2
  28.1 0.4 broadcast_compare_fusion
  28.5 1.5 fusion.5
  30.0 1.4 fusion.7
  31.4 1.6 convolution_convert_fusion
  33.0 0.2 all-gather.4.cloned.1.call-start
  33.3 115.9 %all-gather.6.cloned.1.call-done = bf16[4096,1280]{1,0:T(8,128)(2,1)} async-done(((bf16[512,1280]{1,0:T(8,128)(2,1)}), bf16[4096,1280]{1,0:T(8,128)(2,1)}) %all-gather.6.cloned.1.call-update) | async-done | bytes 10485776 | tf_op jit(solution)/shard_map/all_gather | solution.py:92
  149.2 6.2 %reduce_sum.110 = bf16[512,1280]{1,0:T(8,128)(2,1)S(1)} reduce(bf16[8,512,1280]{2,1,0:T(8,128)(2,1)} %bitcast.37, bf16[]{:T(256)} %constant.100.clone.1), dimensions={0}, to_apply=%region_8.9 | reduce | flops 4587520 | bytes 11796482 | tf_op jit(solution)/shard_map/reduce_sum | solution.py:92
  155.4 2.2 fusion.11
  157.7 0.3 copy-done.2
  157.9 0.6 multiply_reduce_fusion
  158.5 1.5 multiply_convert_fusion
  160.0 2.5 reshape.198
  162.6 1.2 convolution_convert_fusion.4
  163.8 0.6 fusion.32
  164.5 1.3 fusion.30
  170.6 70.6 %all-gather.4.cloned.1.call-done = bf16[8192,160]{0,1:T(8,128)(2,1)} async-done(((bf16[128,160]{0,1:T(8,128)(2,1)}), bf16[8192,160]{0,1:T(8,128)(2,1)}) %all-gather.4.cloned.1.call-update) | async-done | bytes 2621456 | tf_op jit(solution)/shard_map/all_gather | solution.py:104
  241.2 4.4 %fusion.8 = bf16[248,160]{0,1:T(8,128)(2,1)} fusion(bf16[8192,160]{0,1:T(8,128)(2,1)} %all-gather.4.cloned.1.call-done, s32[8192]{0:T(1024)S(1)} %iota_subtract_fusion, pred[8192]{0:T(1024)(128)(4,1)S(1)} %iota_compare_fusion.6), kind=kOutput, calls=%fused_computation.21 | convolution fusion | flops 654220032 | bytes 2741760 | tf_op jit(solution)/shard_map/dot_general | solution.py:109
  (33 shorter events, 0.2 us)
Async XLA Ops:
  6.5 156.0 %copy-start = (bf16[160,5120]{1,0:T(8,128)(2,1)S(1)}, bf16[160,5120]{1,0:T(8,128)(2,1)}, u32[]{:S(2)}) copy-start(bf16[160,5120]{1,0:T(8,128)(2,1)} %param.15) | copy-start | bytes 4915204
  6.5 3.7 %copy-start.4 = (bf16[64,1280]{1,0:T(8,128)(2,1)S(1)}, bf16[64,1280]{1,0:T(8,128)(2,1)}, u32[]{:S(2)}) copy-start(bf16[64,1280]{1,0:T(8,128)(2,1)} %param.12) | copy-start | bytes 491524
  6.5 142.6 %all-gather.6.cloned.1.call-start = ((), (), s32[]{:S(2)}) async-start(), calls=%async_computation.1 | async-start | bytes 11796480 | tf_op jit(solution)/shard_map/all_gather | solution.py:92
  10.9 1.5 copy-start.1
  11.3 1.8 copy-start.8
  11.4 11.2 %copy-start.5 = (s32[512]{0:T(512)S(1)}, s32[512]{0:T(512)}, u32[]{:S(2)}) copy-start(s32[512]{0:T(512)} %param.16) | copy-start | bytes 6148
  13.7 14.7 %collective-permute-start.2 = (bf16[512,160]{0,1:T(8,128)(2,1)S(1)}, bf16[512,160]{0,1:T(8,128)(2,1)S(1)}, u32[]{:S(2)}, u32[]{:S(2)}) collective-permute-start(bf16[512,160]{0,1:T(8,128)(2,1)S(1)} %convolution_convert_fusion.1), channel_id=1, source_target_pairs={{0,1},{1,0},{2,3},{3,2},{4,5},{5,4},{6,7},{7,6},{8,9},{9,8},{10,11... | collective-permute-start | bytes 491528 | tf_op jit(solution)/shard_map/ppermute | solution.py:12
  22.5 5.5 %collective-permute-start.1 = (bf16[512]{0:T(512)(128)(2,1)S(1)}, bf16[512]{0:T(512)(128)(2,1)S(1)}, u32[]{:S(2)}, u32[]{:S(2)}) collective-permute-start(bf16[512]{0:T(512)(128)(2,1)S(1)} %get-tuple-element.8), channel_id=1, source_target_pairs={{0,1},{1,0},{2,3},{3,2},{4,5},{5,4},{6,7},{7,6},{8,9},{9,8},{10,11... | collective-permute-start | bytes 3080 | tf_op jit(solution)/shard_map/ppermute | solution.py:12
  25.0 4.9 %collective-permute-start = (bf16[512,160]{0,1:T(8,128)(2,1)S(1)}, bf16[512,160]{0,1:T(8,128)(2,1)S(1)}, u32[]{:S(2)}, u32[]{:S(2)}) collective-permute-start(bf16[512,160]{0,1:T(8,128)(2,1)S(1)} %convolution_convert_fusion.3), channel_id=1, source_target_pairs={{0,1},{1,0},{2,3},{3,2},{4,5},{5,4},{6,7},{7,6},{8,9},{9,8},{10,11... | collective-permute-start | bytes 491528 | tf_op jit(solution)/shard_map/ppermute | solution.py:12
  30.0 1.4 copy-start.3
  33.0 208.2 %all-gather.4.cloned.1.call-start = ((), (), s32[]{:S(2)}) async-start(), calls=%async_computation | async-start | bytes 2662400 | tf_op jit(solution)/shard_map/all_gather | solution.py:104
  155.4 2.5 %copy-start.2 = (f32[512,1280]{1,0:T(8,128)S(1)}, f32[512,1280]{1,0:T(8,128)}, u32[]{:S(2)}) copy-start(f32[512,1280]{1,0:T(8,128)} %copy-done.1) | copy-start | bytes 7864324
  160.0 3.8 %copy-start.9 = (s32[64]{0:T(128)S(1)}, s32[64]{0:T(128)}, u32[]{:S(2)}) copy-start(s32[64]{0:T(128)} %param.19) | copy-start | bytes 772
  160.0 4.4 %copy-start.6 = (s32[64]{0:T(128)S(1)}, s32[64]{0:T(128)}, u32[]{:S(2)}) copy-start(s32[64]{0:T(128)} %param.18) | copy-start | bytes 772
  160.0 4.4 %copy-start.7 = (s32[64,2]{0,1:T(2,128)S(1)}, s32[64,2]{0,1:T(2,128)}, u32[]{:S(2)}) copy-start(s32[64,2]{0,1:T(2,128)} %param.17) | copy-start | bytes 1540
Sparse Core Ops, SparseCore 0:
  33.1 115.9 all-gather.5
  163.9 77.2 all-gather.3
